TPU v7x, 512 devices: a whole 4x8x8 slice. The times are simulated.
512 devices in a mesh: pts: 32 (over z_lo, y, core), ctr: 16 (over z_hi, x).
Axes of the slice: x: 4, y: 8, z: 8 (z_hi: 4, z_lo: 2; z = z_hi * 2 + z_lo), core: 2. Of those that a mesh axis runs over, the one named last changes fastest.
Arguments:
- points: bfloat16 [8192, 256], P('pts', 'ctr'), may hold values from -6 to 6
- centres: bfloat16 [8192, 256], P('ctr', 'pts'), may hold values from -6 to 6
- precisions: float32 [256], replicated, may hold values from 9.765625e-05 to 0.01953125
- targets: bfloat16 [8192, 128], P('pts', 'ctr'), may hold values from -6 to 6
Outputs:
- coefficients: float32 [8192, 128], P('ctr')
- residual: float32 [8192, 128], P('ctr')
All inputs are finite; a program needn't handle non-finite values.
Results may differ from a plain program's by a relative error of at most 0.0033.
Values may be sent and summed in bfloat16 or wider, within the bound.
No kernel may reach another device: no remote copies, remote signals or barrier semaphores. Data moves between devices by JAX's collectives and lax.ppermute only.
A program may use at most 64 MiB of HBM per device.

v0:
```python
import math
import jax
import jax.numpy as jnp
from jax import lax
from jax.sharding import PartitionSpec as P

FEATURES = 256
BLOCK = 512
NEWTON = 2
ridge_weight = 0.05
jitter_term = 0.1
highest = lax.Precision.HIGHEST


def block_product(matrices, vectors):
    grouped = vectors.reshape(matrices.shape[0], matrices.shape[1], vectors.shape[1])
    return jnp.einsum("bij,bjr->bir", matrices, grouped, precision=highest).reshape(vectors.shape)


def batched(left, right):
    return jnp.einsum("bij,bjk->bik", left, right, precision=highest)


def on_device(points, centres, precisions, targets):
    full_points, full_targets = (
        lax.all_gather(points, "ctr", axis=1, tiled=True),
        lax.all_gather(targets, "ctr", axis=1, tiled=True),
    )
    full_centres = lax.all_gather(centres, "pts", axis=1, tiled=True)
    total = points.shape[0] * lax.axis_size("pts")
    count_blocks = centres.shape[0] // BLOCK
    point_float = full_points.astype(jnp.float32)
    point_square = jnp.sum(precisions * point_float * point_float, axis=1)
    scaled_points = (point_float * precisions).astype(jnp.bfloat16)
    centre_float = full_centres.astype(jnp.float32)
    centre_square = jnp.sum(precisions * centre_float * centre_float, axis=1)
    scaled_centres = (centre_float * precisions).astype(jnp.bfloat16)
    cross_term = lax.dot_general(
        scaled_points, full_centres, (((1,), (1,)), ((), ())), preferred_element_type=jnp.float32
    )
    kernel_tile = jnp.exp(-(point_square[:, None] + centre_square[None, :] - 2.0 * cross_term))
    grouped_scaled = scaled_centres.reshape(count_blocks, BLOCK, FEATURES)
    grouped_centres = full_centres.reshape(count_blocks, BLOCK, FEATURES)
    block_cross = jnp.einsum(
        "bif,bjf->bij", grouped_scaled, grouped_centres, preferred_element_type=jnp.float32
    )
    grouped_square = centre_square.reshape(count_blocks, BLOCK)
    similar = jnp.exp(
        -(grouped_square[:, :, None] + grouped_square[:, None, :] - 2.0 * block_cross)
    )
    identity = jnp.eye(BLOCK, dtype=jnp.float32)
    blocks = 0.5 * (similar + jnp.swapaxes(similar, 1, 2)) + jitter_term * identity
    scale = jnp.sqrt(jnp.sum(blocks * blocks, axis=(1, 2)))
    current_y = blocks / scale[:, None, None]
    current_z = jnp.broadcast_to(identity, blocks.shape)
    width = BLOCK // lax.axis_size("pts")
    first = lax.axis_index("pts") * width
    rows_iota = lax.broadcasted_iota(jnp.int32, (BLOCK, width), 0)
    cols_iota = lax.broadcasted_iota(jnp.int32, (BLOCK, width), 1)
    identity_cols = jnp.where(rows_iota == cols_iota + first, 1.0, 0.0).astype(jnp.float32)
    for newton_step in range(NEWTON):
        y_columns = lax.dynamic_slice_in_dim(current_y, first, width, 2)
        factor = 3.0 * identity_cols - batched(current_z, y_columns)
        next_y = 0.5 * batched(current_y, factor)
        next_z = 0.5 * batched(current_z, factor)
        if newton_step + 1 < NEWTON:
            current_y, current_z = (
                lax.all_gather(next_y, "pts", axis=2, tiled=True),
                lax.all_gather(next_z, "pts", axis=2, tiled=True),
            )
        else:
            current_z = lax.all_gather(next_z, "pts", axis=2, tiled=True)
    target_float = full_targets.astype(jnp.float32)
    right_part = lax.dot_general(
        kernel_tile, target_float, (((0,), (0,)), ((), ())), precision=highest
    )
    right = lax.psum(right_part, "pts") / math.sqrt(total)
    gradient = block_product(current_z, right)
    residual = gradient
    direction = residual
    norm_now = lax.psum(jnp.sum(residual * residual, axis=0), "ctr")
    spread = block_product(current_z, direction)
    values = lax.psum(
        jnp.dot(kernel_tile, spread, precision=highest).astype(jnp.bfloat16), "ctr"
    ).astype(jnp.float32)
    back_part = lax.dot_general(kernel_tile, values, (((0,), (0,)), ((), ())), precision=highest)
    back = lax.psum(back_part, "pts")
    normal = back / total + ridge_weight * block_product(blocks, spread)
    image = block_product(current_z, normal)
    curve = lax.psum(jnp.sum(direction * image, axis=0), "ctr")
    step_size = norm_now / curve
    solution = step_size * direction
    residual = residual - step_size * image
    return (block_product(current_z, solution), residual)


def solution(mesh):
    in_specs = (P("pts", "ctr"), P("ctr", "pts"), P(), P("pts", "ctr"))
    out_specs = (P("ctr", None), P("ctr", None))
    return jax.shard_map(
        on_device, mesh=mesh, in_specs=in_specs, out_specs=out_specs, check_vma=False
    )
```

profile of v0, /device:TPU:64, one launch (start us, length us, event | category | flops | bytes accessed | tf_op | source)
XLA Modules:
  0.0 937.3 jit_solution(13510429586584781246)
XLA Ops:
  7.2 0.0 all-gather.9.cloned.1.call-start
  7.2 33.9 %all_gather.18 = bf16[512,256]{0,1:T(8,128)(2,1)S(1)} all-gather(bf16[512,8]{0,1:T(8,128)(2,1)} %param.5), channel_id=1, replica_groups=mesh['pts'=32,'ctr'=16] {'pts'}, dimensions={1}, use_global_device_ids=true | all-gather | bytes 270336 | tf_op jit(solution)/shard_map/all_gather | solution.py:29
  41.1 0.2 fusion.12
  41.3 0.5 fusion.3
  41.7 0.3 copy.6
  42.1 0.9 multiply_reduce_fusion
  43.7 0.2 broadcast_divide_fusion
  43.9 0.6 convolution_subtract_fusion.1
  44.5 1.6 convolution_multiply_fusion.4
  46.1 0.0 all-gather.9.cloned.1.call-update
  46.1 0.0 all-gather.7.cloned.1.call-start
  46.2 1.0 convolution_multiply_fusion.5
  47.1 0.0 all-gather.7.cloned.1.call-update
  47.2 0.0 copy-start.5
  47.2 0.0 all-reduce.5.cloned.1.call-start
  47.2 0.6 copy-done.7
  47.8 49.5 %all_gather.23 = bf16[256,128]{0,1:T(8,128)(2,1)S(1)} all-gather(bf16[256,8]{0,1:T(8,128)(2,1)S(1)} %copy-done.7), channel_id=1, replica_groups=mesh['pts'=32,'ctr'=16] {'ctr'}, dimensions={1}, use_global_device_ids=true | all-gather | bytes 69632 | tf_op jit(solution)/shard_map/all_gather | solution.py:27
  97.3 38.6 %all_gather.22 = bf16[256,256]{0,1:T(8,128)(2,1)S(1)} all-gather(bf16[256,16]{0,1:T(8,128)(2,1)S(1)} %copy-done.5), channel_id=1, replica_groups=mesh['pts'=32,'ctr'=16] {'ctr'}, dimensions={1}, use_global_device_ids=true | all-gather | bytes 139264 | tf_op jit(solution)/shard_map/all_gather | solution.py:26
  136.0 0.1 fusion.13
  136.1 0.4 fusion.6
  136.5 0.8 copy-done.1
  137.2 1.3 fusion.29
  138.5 0.0 all-reduce.5.cloned.1.call-update
  138.6 0.0 all-gather.11.cloned.1.call-start
  138.6 0.0 all-gather.9.cloned.1.call-done
  138.6 42.3 %all-gather.7.cloned.1.call-done = f32[512,512]{0,1:T(8,128)} async-done(((f32[512,16]{0,1:T(8,128)}), f32[512,512]{0,1:T(8,128)}) %all-gather.7.cloned.1.call-update) | async-done | bytes 1048592 | tf_op jit(solution)/shard_map/all_gather | solution.py:69
  180.9 2.0 convolution_subtract_fusion
  182.9 1.3 convolution_multiply_fusion.3
  184.2 0.0 all-gather.11.cloned.1.call-update
  184.2 0.0 all-reduce.7.cloned.1.call-start
  184.3 229.5 %all-reduce.5.cloned.1.call-done = f32[512,128]{1,0:T(8,128)} async-done(((f32[512,128]{1,0:T(8,128)}), f32[512,128]{1,0:T(8,128)}) %all-reduce.5.cloned.1.call-update) | async-done | bytes 262160 | tf_op jit(solution)/shard_map/psum | solution.py:77
  413.8 67.1 %all-gather.11.cloned.1.call-done = f32[512,512]{0,1:T(8,128)} async-done(((f32[512,16]{0,1:T(8,128)}), f32[512,512]{0,1:T(8,128)}) %all-gather.11.cloned.1.call-update) | async-done | bytes 1048592 | tf_op jit(solution)/shard_map/all_gather | solution.py:72
  480.9 3.2 fusion.17
  484.1 1.8 fusion.30
  485.9 0.0 copy-start.4
  485.9 0.7 copy-done.4
  486.6 1.2 convolution_convert_fusion
  487.8 0.0 all-reduce.7.cloned.1.call-update
  487.8 0.2 all-reduce.9.cloned.1.call-start
  488.1 160.2 %all-reduce.7.cloned.1.call-done = bf16[256,128]{1,0:T(8,128)(2,1)} async-done(((bf16[256,128]{1,0:T(8,128)(2,1)}), bf16[256,128]{1,0:T(8,128)(2,1)}) %all-reduce.7.cloned.1.call-update) | async-done | bytes 65552 | tf_op jit(solution)/shard_map/psum | solution.py:83
  648.2 2.4 fusion.31
  650.6 0.0 all-reduce.9.cloned.1.call-update
  650.6 227.8 %all-reduce.9.cloned.1.call-done = f32[512,128]{1,0:T(8,128)} async-done(((f32[512,128]{1,0:T(8,128)}), f32[512,128]{1,0:T(8,128)}) %all-reduce.9.cloned.1.call-update) | async-done | bytes 262160 | tf_op jit(solution)/shard_map/psum | solution.py:87
  878.4 2.0 fusion.7
  880.4 1.8 multiply_reduce_fusion.1
  882.2 44.9 %all-reduce = (f32[128]{0:T(128)S(1)}, f32[128]{0:T(128)S(1)}) all-reduce(f32[128]{0:T(128)S(1)} %get-tuple-element.3, f32[128]{0:T(128)S(1)} %get-tuple-element.2), channel_id=1, replica_groups=mesh['pts'=32,'ctr'=16] {'ctr'}, use_global_device_ids=true, to_apply=%region_5.6 | all-reduce | flops 256 | bytes 2048 | tf_op jit(solution)/shard_map/psum | solution.py:81
  927.2 0.7 multiply_subtract_fusion
  927.9 2.5 fusion.15
  (13 shorter events, 0.0 us)
Async XLA Ops:
  7.2 131.5 %all-gather.9.cloned.1.call-start = ((), (), s32[]{:S(2)}) async-start(), calls=%async_computation.4 | async-start | bytes 1081344 | tf_op jit(solution)/shard_map/all_gather | solution.py:68
  7.2 33.9 %copy-start.6 = (f32[256]{0:T(256)S(1)}, f32[256]{0:T(256)}, u32[]{:S(2)}) copy-start(f32[256]{0:T(256)} %param.6) | copy-start | bytes 3076
  46.1 134.8 %all-gather.7.cloned.1.call-start = ((), (), s32[]{:S(2)}) async-start(), calls=%async_computation.3 | async-start | bytes 1081344 | tf_op jit(solution)/shard_map/all_gather | solution.py:69
  47.1 0.7 copy-start.7
  47.2 50.2 %copy-start.5 = (bf16[256,16]{0,1:T(8,128)(2,1)S(1)}, bf16[256,16]{0,1:T(8,128)(2,1)}, u32[]{:S(2)}) copy-start(bf16[256,16]{0,1:T(8,128)(2,1)} %param.4) | copy-start | bytes 24580
  47.2 366.6 %all-reduce.5.cloned.1.call-start = ((), (), s32[]{:S(2)}) async-start(), calls=%async_computation | async-start | bytes 524288 | tf_op jit(solution)/shard_map/psum | solution.py:77
  136.4 0.8 copy-start.1
  138.6 342.3 %all-gather.11.cloned.1.call-start = ((), (), s32[]{:S(2)}) async-start(), calls=%async_computation.5 | async-start | bytes 1081344 | tf_op jit(solution)/shard_map/all_gather | solution.py:72
  180.9 2.0 copy-start.3
  184.2 464.0 %all-reduce.7.cloned.1.call-start = ((), (), s32[]{:S(2)}) async-start(), calls=%async_computation.1 | async-start | bytes 131072 | tf_op jit(solution)/shard_map/psum | solution.py:83
  480.9 3.2 copy-start
  484.1 2.5 copy-start.2
  485.9 0.7 copy-start.4
  487.8 390.5 %all-reduce.9.cloned.1.call-start = ((), (), s32[]{:S(2)}) async-start(), calls=%async_computation.2 | async-start | bytes 524288 | tf_op jit(solution)/shard_map/psum | solution.py:87
Sparse Core Ops, SparseCore 0:
  46.2 65.9 all-gather.8
  114.9 65.9 all-gather.6
  184.4 229.2 all-reduce.4
  416.3 64.5 all-gather.10
  488.0 160.2 all-reduce.6
  651.5 226.7 all-reduce.8
where the time goes:
time: 938 us; the launch traced here: 937 us
  waiting for transfers between devices  727 us (78%)
  blocking collectives  167 us (18%)
  matrix products  23.4 us (2%)
  between operations  15 us (2%)
    psum x1, waiting for transfers between devices, on_device(): right = lax.psum(right_part, 'pts') / math.sqrt(total)  229 us
    psum x1, waiting for transfers between devices, on_device(): back = lax.psum(back_part, 'pts')  228 us
    psum x1, waiting for transfers between devices, on_device(): lax.psum(jnp.dot(kernel_tile, spread, precision=highest).astype(jnp.bfloa...  160 us
    all_gather x1, waiting for transfers between devices, on_device(): current_z = lax.all_gather(next_z, 'pts', axis=2, tiled=True)  67.1 us
    all_gather x1, blocking collectives, on_device(): lax.all_gather(targets, 'ctr', axis=1, tiled=True)  49.5 us
    psum x1, blocking collectives, on_device(): norm_now = lax.psum(jnp.sum(residual * residual, axis=0), 'ctr')  44.9 us
    all_gather x1, waiting for transfers between devices, on_device(): lax.all_gather(next_z, 'pts', axis=2, tiled=True)  42.3 us
    all_gather x1, blocking collectives, on_device(): lax.all_gather(points, 'ctr', axis=1, tiled=True)  38.6 us
  transfers between devices with their start and end apart: 6, of which 5 were waited for; matrix products, arithmetic and copies ran while one was open for 1% of the time, Pallas kernels for 0%

commit v1 on v0

--- a/solution.py
+++ b/solution.py
@@ -84,7 +84,7 @@
         jnp.dot(kernel_tile, spread, precision=highest).astype(jnp.bfloat16), "ctr"
     ).astype(jnp.float32)
     back_part = lax.dot_general(kernel_tile, values, (((0,), (0,)), ((), ())), precision=highest)
-    back = lax.psum(back_part, "pts")
+    back = jnp.sum(lax.all_gather(back_part, "pts"), axis=0)
     normal = back / total + ridge_weight * block_product(blocks, spread)
     image = block_product(current_z, normal)
     curve = lax.psum(jnp.sum(direction * image, axis=0), "ctr")

time: 938 us -> 790 us (0.84)
  the two profiles are of different devices: /device:TPU:64 before, /device:TPU:16 now
where the time goes in v1:
time: 790 us
  waiting for transfers between devices  571 us (72%)
  blocking collectives  166 us (21%)
  matrix products  27.4 us (3%)
  between operations  14.9 us (2%)
    psum x1, waiting for transfers between devices, on_device(): right = lax.psum(right_part, 'pts') / math.sqrt(total)  223 us
    psum x1, waiting for transfers between devices, on_device(): lax.psum(jnp.dot(kernel_tile, spread, precision=highest).astype(jnp.bfloa...  160 us
    all_gather x1, waiting for transfers between devices, on_device(): current_z = lax.all_gather(next_z, 'pts', axis=2, tiled=True)  72.7 us
    all_gather x1, waiting for transfers between devices, on_device(): back = jnp.sum(lax.all_gather(back_part, 'pts'), axis=0)  71.9 us
    all_gather x1, blocking collectives, on_device(): lax.all_gather(targets, 'ctr', axis=1, tiled=True)  48.5 us
    psum x1, blocking collectives, on_device(): norm_now = lax.psum(jnp.sum(residual * residual, axis=0), 'ctr')  45.7 us
    all_gather x1, waiting for transfers between devices, on_device(): lax.all_gather(next_y, 'pts', axis=2, tiled=True)  43.7 us
    all_gather x1, blocking collectives, on_device(): lax.all_gather(points, 'ctr', axis=1, tiled=True)  38.7 us
  transfers between devices with their start and end apart: 6, of which 5 were waited for; matrix products, arithmetic and copies ran while one was open for 1% of the time, Pallas kernels for 0%

profile of v1, /device:TPU:16, one launch (start us, length us, event | category | flops | bytes accessed | tf_op | source)
XLA Modules:
  0.0 789.7 jit_solution(16747300340248054417)
XLA Ops:
  7.2 0.0 copy-start.4
  7.2 0.0 all-gather.9.cloned.1.call-start
  7.3 33.5 %all_gather.24 = bf16[512,256]{0,1:T(8,128)(2,1)S(1)} all-gather(bf16[512,8]{0,1:T(8,128)(2,1)} %param.5), channel_id=1, replica_groups=mesh['pts'=32,'ctr'=16] {'pts'}, dimensions={1}, use_global_device_ids=true | all-gather | bytes 270336 | tf_op jit(solution)/shard_map/all_gather | solution.py:29
  40.8 0.8 fusion.12
  41.6 1.1 fusion.3
  42.7 0.3 copy.6
  43.1 0.9 multiply_reduce_fusion
  44.7 0.2 broadcast_divide_fusion
  45.0 0.6 convolution_subtract_fusion.1
  45.5 1.0 convolution_multiply_fusion.5
  46.5 0.0 all-gather.9.cloned.1.call-update
  46.5 0.0 all-gather.11.cloned.1.call-start
  46.6 1.6 convolution_multiply_fusion.4
  48.2 0.0 all-gather.11.cloned.1.call-update
  48.2 0.0 all-reduce.4.cloned.1.call-start
  48.2 48.5 %all_gather.29 = bf16[256,128]{0,1:T(8,128)(2,1)S(1)} all-gather(bf16[256,8]{0,1:T(8,128)(2,1)S(1)} %copy-done.5), channel_id=1, replica_groups=mesh['pts'=32,'ctr'=16] {'ctr'}, dimensions={1}, use_global_device_ids=true | all-gather | bytes 69632 | tf_op jit(solution)/shard_map/all_gather | solution.py:27
  96.7 38.7 %all_gather.28 = bf16[256,256]{0,1:T(8,128)(2,1)S(1)} all-gather(bf16[256,16]{0,1:T(8,128)(2,1)S(1)} %copy-done.3), channel_id=1, replica_groups=mesh['pts'=32,'ctr'=16] {'ctr'}, dimensions={1}, use_global_device_ids=true | all-gather | bytes 139264 | tf_op jit(solution)/shard_map/all_gather | solution.py:26
  135.4 0.1 fusion.13
  135.6 0.3 fusion.6
  135.9 0.8 copy-done.1
  136.7 1.3 fusion.29
  138.0 0.0 all-reduce.4.cloned.1.call-update
  138.0 0.0 all-gather.13.cloned.1.call-start
  138.1 0.0 all-gather.9.cloned.1.call-done
  138.1 43.7 %all-gather.11.cloned.1.call-done = f32[512,512]{0,1:T(8,128)} async-done(((f32[512,16]{0,1:T(8,128)}), f32[512,512]{0,1:T(8,128)}) %all-gather.11.cloned.1.call-update) | async-done | bytes 1048592 | tf_op jit(solution)/shard_map/all_gather | solution.py:68
  181.9 1.9 convolution_subtract_fusion
  183.7 2.5 convolution_multiply_fusion.3
  186.2 0.0 all-gather.13.cloned.1.call-update
  186.3 0.0 all-reduce.6.cloned.1.call-start
  186.3 222.8 %all-reduce.4.cloned.1.call-done = f32[512,128]{1,0:T(8,128)} async-done(((f32[512,128]{1,0:T(8,128)}), f32[512,128]{1,0:T(8,128)}) %all-reduce.4.cloned.1.call-update) | async-done | bytes 262160 | tf_op jit(solution)/shard_map/psum | solution.py:77
  409.1 72.7 %all-gather.13.cloned.1.call-done = f32[512,512]{0,1:T(8,128)} async-done(((f32[512,16]{0,1:T(8,128)}), f32[512,512]{0,1:T(8,128)}) %all-gather.13.cloned.1.call-update) | async-done | bytes 1048592 | tf_op jit(solution)/shard_map/all_gather | solution.py:72
  481.8 3.2 fusion.17
  485.0 3.0 fusion.30
  488.0 0.0 copy-start.2
  488.0 0.7 copy-done.2
  488.7 2.3 convolution_convert_fusion
  491.0 0.0 all-reduce.6.cloned.1.call-update
  491.0 0.2 all-gather.15.cloned.1.call-start
  491.2 159.9 %all-reduce.6.cloned.1.call-done = bf16[256,128]{1,0:T(8,128)(2,1)} async-done(((bf16[256,128]{1,0:T(8,128)(2,1)}), bf16[256,128]{1,0:T(8,128)(2,1)}) %all-reduce.6.cloned.1.call-update) | async-done | bytes 65552 | tf_op jit(solution)/shard_map/psum | solution.py:83
  651.2 2.4 fusion.31
  653.5 0.0 all-gather.15.cloned.1.call-update
  653.6 71.9 %all-gather.15.cloned.1.call-done = f32[16384,128]{1,0:T(8,128)} async-done(((f32[512,128]{1,0:T(8,128)}), f32[16384,128]{1,0:T(8,128)}) %all-gather.15.cloned.1.call-update) | async-done | bytes 8388624 | tf_op jit(solution)/shard_map/all_gather | solution.py:87
  725.5 4.5 reduce_sum.58
  730.0 2.0 fusion.7
  732.0 1.8 multiply_reduce_fusion.1
  733.8 45.7 %all-reduce = (f32[128]{0:T(128)S(1)}, f32[128]{0:T(128)S(1)}) all-reduce(f32[128]{0:T(128)S(1)} %get-tuple-element.3, f32[128]{0:T(128)S(1)} %get-tuple-element.2), channel_id=1, replica_groups=mesh['pts'=32,'ctr'=16] {'ctr'}, use_global_device_ids=true, to_apply=%region_5.6 | all-reduce | flops 256 | bytes 2048 | tf_op jit(solution)/shard_map/psum | solution.py:81
  779.6 0.7 multiply_subtract_fusion
  780.3 2.5 fusion.15
  (10 shorter events, 0.0 us)
Async XLA Ops:
  7.2 128.3 %copy-start.4 = (f32[256]{0:T(256)S(1)}, f32[256]{0:T(256)}, u32[]{:S(2)}) copy-start(f32[256]{0:T(256)} %param.6) | copy-start | bytes 3076
  7.2 41.1 %copy-start.5 = (bf16[256,8]{0,1:T(8,128)(2,1)S(1)}, bf16[256,8]{0,1:T(8,128)(2,1)}, u32[]{:S(2)}) copy-start(bf16[256,8]{0,1:T(8,128)(2,1)} %param.7) | copy-start | bytes 12292
  7.2 89.6 %copy-start.3 = (bf16[256,16]{0,1:T(8,128)(2,1)S(1)}, bf16[256,16]{0,1:T(8,128)(2,1)}, u32[]{:S(2)}) copy-start(bf16[256,16]{0,1:T(8,128)(2,1)} %param.4) | copy-start | bytes 24580
  7.2 130.9 %all-gather.9.cloned.1.call-start = ((), (), s32[]{:S(2)}) async-start(), calls=%async_computation.2 | async-start | bytes 1081344 | tf_op jit(solution)/shard_map/all_gather | solution.py:69
  46.5 135.4 %all-gather.11.cloned.1.call-start = ((), (), s32[]{:S(2)}) async-start(), calls=%async_computation.3 | async-start | bytes 1081344 | tf_op jit(solution)/shard_map/all_gather | solution.py:68
  48.2 361.0 %all-reduce.4.cloned.1.call-start = ((), (), s32[]{:S(2)}) async-start(), calls=%async_computation | async-start | bytes 524288 | tf_op jit(solution)/shard_map/psum | solution.py:77
  135.9 0.8 copy-start.1
  138.0 343.8 %all-gather.13.cloned.1.call-start = ((), (), s32[]{:S(2)}) async-start(), calls=%async_computation.4 | async-start | bytes 1081344 | tf_op jit(solution)/shard_map/all_gather | solution.py:72
  186.3 464.9 %all-reduce.6.cloned.1.call-start = ((), (), s32[]{:S(2)}) async-start(), calls=%async_computation.1 | async-start | bytes 131072 | tf_op jit(solution)/shard_map/psum | solution.py:83
  481.8 250.2 %copy-start = (f32[512,512]{0,1:T(8,128)S(1)}, f32[512,512]{0,1:T(8,128)}, u32[]{:S(2)}) copy-start(f32[512,512]{0,1:T(8,128)} %all-gather.13.cloned.1.call-done) | copy-start | bytes 3145732
  488.0 0.7 copy-start.2
  491.0 234.5 %all-gather.15.cloned.1.call-start = ((), (), s32[]{:S(2)}) async-start(), calls=%async_computation.5 | async-start | bytes 8650752 | tf_op jit(solution)/shard_map/all_gather | solution.py:87
Sparse Core Ops, SparseCore 0:
  46.6 67.1 all-gather.8
  115.9 65.8 all-gather.10
  185.3 223.7 all-reduce.3
  411.7 70.0 all-gather.12
  491.1 160.0 all-reduce.5
  653.7 71.6 all-gather.14
